TPU v7x, 512 devices: a whole 4x8x8 slice. The times are simulated.
512 devices in a mesh: ctx: 32 (over y, z_lo), head: 4 (over x), batch: 4 (over z_hi, core).
Axes of the slice: x: 4, y: 8, z: 8 (z_hi: 2, z_lo: 4; z = z_hi * 4 + z_lo), core: 2. Of those that a mesh axis runs over, the one named last changes fastest.
Arguments:
- queries: bfloat16 [4, 4096, 20, 128], P('batch', 'ctx', 'head'), may hold values from -64 to 64
- key_rows: bfloat16 [4, 4096, 4, 128], P('batch', 'ctx', 'head'), may hold values from -8 to 8
- block_order: int32 [64], replicated, may hold values from 0 to 63, each once
- conv_len: int32 [4], replicated, may hold values from 2048 to 4096
- gate_wq: float32 [128, 128], replicated, may hold values from -32 to 32
- gate_wk: float32 [384, 128], replicated, may hold values from -32 to 32
Outputs:
- teacher_map: float32 [4, 20, 64, 64], P('batch', 'head', 'ctx')
- grad_wq: float32 [128, 128], replicated
- grad_wk: float32 [384, 128], replicated
All inputs are finite; a program needn't handle non-finite values.
Results may differ from a plain program's by a relative error of at most 0.0003.
Values may be sent and summed in bfloat16 or wider, within the bound.
No kernel may reach another device: no remote copies, remote signals or barrier semaphores. Data moves between devices by JAX's collectives and lax.ppermute only.
A program may use at most 64 MiB of HBM per device.

v0:
```python
import math
import jax
import jax.numpy as jnp
from jax import lax
from jax.sharding import PartitionSpec as P

BLK = 64
masked_value = -1e30
norm_epsilon = 1e-06


def score_tile(query_group, key_tile, query_pos, key_pos, length):
    scores = jnp.einsum(
        "rgqd,kgd->gqrk", query_group, key_tile, preferred_element_type=jnp.float32
    ) / math.sqrt(key_tile.shape[-1])
    allowed = (key_pos[None, :] <= query_pos[:, None]) & (key_pos[None, :] < length)
    return (jnp.where(allowed, scores, masked_value), allowed)


def gate_loss(
    weight_query, weight_key, pooled_query, pooled_key, target_map, query_starts, key_starts, length
):
    kv_heads = pooled_key.shape[1]
    group_size = pooled_query.shape[1] // kv_heads
    width_gate = weight_query.shape[1]
    proj_query = jnp.einsum(
        "bhd,de->bhe", pooled_query, weight_query, precision=lax.Precision.HIGHEST
    )
    proj_key = jnp.einsum("bgd,de->bge", pooled_key, weight_key, precision=lax.Precision.HIGHEST)
    unit_query = proj_query * lax.rsqrt(
        jnp.mean(proj_query * proj_query, axis=-1, keepdims=True) + norm_epsilon
    )
    unit_key = proj_key * lax.rsqrt(
        jnp.mean(proj_key * proj_key, axis=-1, keepdims=True) + norm_epsilon
    )
    query_count = unit_query.shape[0]
    unit_query = unit_query.reshape(query_count, kv_heads, group_size, width_gate)
    logits = jnp.einsum(
        "igqe,jge->gqij", unit_query, unit_key, precision=lax.Precision.HIGHEST
    ) / math.sqrt(width_gate)
    logits = logits.reshape(kv_heads * group_size, query_count, unit_key.shape[0])
    allowed = (key_starts[None, :] <= query_starts[:, None]) & (key_starts[None, :] < length)
    weights_exp = jnp.where(allowed[None], jnp.exp(logits), 0.0)
    log_norm = jnp.log(jnp.sum(weights_exp, axis=-1, keepdims=True))
    positive = target_map > 0
    entropy_part = jnp.where(
        positive, target_map * jnp.log(jnp.where(positive, target_map, 1.0)), 0.0
    )
    divergence = entropy_part - target_map * (logits - log_norm)
    return jnp.sum(divergence)


def body(queries, key_rows, block_order, conv_len, gate_wq, gate_wk):
    tok_dev = queries.shape[1]
    head_dev = queries.shape[2]
    kv_dev = key_rows.shape[2]
    head_size = queries.shape[3]
    group_size = head_dev // kv_dev
    block_dev = tok_dev // BLK
    block_count = block_order.shape[0]
    ctx_index = lax.axis_index("ctx")
    length = lax.dynamic_index_in_dim(conv_len, lax.axis_index("batch"), keepdims=False)
    own_blocks = lax.dynamic_slice_in_dim(block_order, ctx_index * block_dev, block_dev)
    offsets = jnp.arange(BLK, dtype=jnp.int32)
    query_pos = (own_blocks[:, None] * BLK + offsets[None, :]).reshape(tok_dev)
    valid_row = (query_pos < length)[:, None]
    query_group = queries[0].reshape(tok_dev, kv_dev, group_size, head_size)

    def tile_loop(update, carry, segment):
        width_keys = segment.shape[1]
        sub_rows = math.gcd(width_keys, 512)
        key_pos = (block_order[:, None] * BLK + offsets[None, :]).reshape(width_keys)

        def advance(step_index, state):
            first = step_index * sub_rows
            key_tile = lax.dynamic_slice_in_dim(segment[0], first, sub_rows, 0)
            tile_pos = lax.dynamic_slice_in_dim(key_pos, first, sub_rows, 0)
            column = first // BLK
            result = update(state, key_tile, tile_pos, column)
            return result

        return lax.fori_loop(0, width_keys // sub_rows, advance, carry)

    def merge_stats(highest, summed, masked, allowed):
        new_high = jnp.maximum(highest, jnp.max(masked, axis=-1))
        fresh = jnp.sum(jnp.where(allowed, jnp.exp(masked - new_high[..., None]), 0.0), axis=-1)
        return (new_high, summed * jnp.exp(highest - new_high) + fresh)

    stats_shape = (kv_dev, group_size, tok_dev)
    start_high = jnp.full(stats_shape, masked_value, jnp.float32)
    start_sum = jnp.zeros(stats_shape, jnp.float32)

    def add_stats(state, key_tile, tile_pos, column):
        masked, allowed = score_tile(query_group, key_tile, query_pos, tile_pos, length)
        return merge_stats(state[0], state[1], masked, allowed)

    highest, summed = tile_loop(
        add_stats, (start_high, start_sum), lax.all_gather(key_rows, "ctx", axis=1, tiled=True)
    )
    log_total = highest + jnp.log(summed)

    def add_pool(state, key_tile, tile_pos, column):
        masked, allowed = score_tile(query_group, key_tile, query_pos, tile_pos, length)
        probs = jnp.where(valid_row, jnp.exp(masked - log_total[..., None]), 0.0)
        tile_max = probs.reshape(
            kv_dev, group_size, block_dev, BLK, key_tile.shape[0] // BLK, BLK
        ).max(axis=(3, 5))
        return lax.dynamic_update_slice_in_dim(state, tile_max, column, 3)

    start_pool = jnp.zeros((kv_dev, group_size, block_dev, block_count), jnp.float32)
    pooled = tile_loop(add_pool, start_pool, lax.all_gather(key_rows, "ctx", axis=1, tiled=True))
    pooled = pooled.reshape(head_dev, block_dev, block_count)
    query_starts = own_blocks * BLK
    valid_block = (query_starts < length)[None, :, None]
    totals = jnp.sum(pooled, axis=-1, keepdims=True)
    target = jnp.where(valid_block, pooled / jnp.where(valid_block, totals, 1.0), 0.0)
    key_local = key_rows[0].reshape(block_dev, BLK, kv_dev, head_size)
    pooled_local = jnp.concatenate(
        [
            jnp.max(key_local, axis=1).astype(jnp.float32),
            jnp.min(key_local, axis=1).astype(jnp.float32),
            jnp.mean(key_local, axis=1, dtype=jnp.float32),
        ],
        axis=-1,
    )
    pooled_all = lax.all_gather(pooled_local, "ctx", axis=0, tiled=True)
    pooled_query = jnp.mean(
        queries[0].reshape(block_dev, BLK, head_dev, head_size), axis=1, dtype=jnp.float32
    )
    key_starts = block_order * BLK

    def local_loss(weight_query, weight_key):
        return gate_loss(
            weight_query,
            weight_key,
            pooled_query,
            pooled_all,
            target,
            query_starts,
            key_starts,
            length,
        )

    loss_value, pullback = jax.vjp(local_loss, gate_wq, gate_wk)
    grad_query, grad_key = pullback(jnp.ones((), jnp.float32))
    grad_query, grad_key = lax.psum((grad_query, grad_key), ("ctx", "head", "batch"))
    return (target[None], grad_query, grad_key)


def solution(mesh):
    in_specs = (
        P("batch", "ctx", "head", None),
        P("batch", "ctx", "head", None),
        P(),
        P(),
        P(),
        P(),
    )
    out_specs = (P("batch", "head", "ctx", None), P(), P())
    return jax.shard_map(body, mesh=mesh, in_specs=in_specs, out_specs=out_specs, check_vma=False)
```

profile of v0, /device:TPU:23, one launch (start us, length us, event | category | flops | bytes accessed | tf_op | source)
XLA Modules:
  0.0 550.4 jit_solution(3898082681139945655)
XLA Ops:
  10.4 56.8 %all_gather.8 = f32[64,1,384]{2,1,0:T(1,128)S(1)} all-gather(f32[2,1,384]{2,1,0:T(1,128)S(1)} %pad_maximum_fusion), channel_id=1, replica_groups=mesh['ctx'=32,'head'=4,'batch'=4] {'ctx'}, dimensions={0}, use_global_device_ids=true | all-gather | bytes 101376 | tf_op jit(solution)/shard_map/all_gather | solution.py:126
  68.4 1.4 broadcast_compare_fusion.4
  74.0 63.9 %all-gather.2.cloned.1.call-done = bf16[1,4096,1,128]{3,1,2,0:T(8,128)(2,1)} async-done(((bf16[1,128,1,128]{3,1,2,0:T(8,128)(2,1)}), bf16[1,4096,1,128]{3,1,2,0:T(8,128)(2,1)}) %all-gather.2.cloned.1.call-update) | async-done | bytes 1048592 | tf_op jit(solution)/shard_map/all_gather | solution.py:111
  137.8 22.0 %while.33 = (s32[]{:T(128)}, f32[1,5,128]{2,1,0:T(8,128)S(1)}, f32[1,5,128]{2,1,0:T(8,128)S(1)}, s32[4096]{0:T(1024)S(1)}, s32[]{:T(128)}, /*index=5*/bf16[1,409...) while((s32[]{:T(128)}, f32[1,5,128]{2,1,0:T(8,128)S(1)}, ...), condition=%wide.region_3.4_spmd.clone, body=%wide.region_0.3_spmd.clone.sunk | while | flops 85987080 | bytes 3155650 | solution.py:82
  159.9 74.3 %while.34 = (s32[]{:T(128)}, f32[1,5,2,64]{3,2,1,0:T(2,128)S(1)}, s32[4096]{0:T(1024)S(1)}, s32[]{:T(128)}, bf16[1,4096,1,128]{3,1,2,0:T(8,128)(2,1)}, /*index=5...) while((s32[]{:T(128)}, f32[1,5,2,64]{3,2,1,0:T(2,128)S(1)}, ...), condition=%wide.region_6.7_spmd.clone.clone, body=%wide.region_4.6_spmd.clone.clone.sunk | while | flops 85656376 | bytes 5683170 | solution.py:82
  161.8 2.5 exponential_select_fusion.2
  164.3 2.8 reshape.363
  170.5 2.5 exponential_select_fusion.2
  173.0 2.8 reshape.363
  179.9 2.5 exponential_select_fusion.2
  182.4 2.8 reshape.363
  189.3 2.5 exponential_select_fusion.2
  191.8 2.8 reshape.363
  198.6 2.5 exponential_select_fusion.2
  201.1 2.8 reshape.363
  208.0 2.5 exponential_select_fusion.2
  210.5 2.8 reshape.363
  217.4 2.5 exponential_select_fusion.2
  219.9 2.8 reshape.363
  226.8 2.5 exponential_select_fusion.2
  229.3 2.8 reshape.363
  238.2 302.2 %all-reduce.3.cloned.1.call-done = (f32[128,128]{1,0:T(8,128)}, f32[384,128]{1,0:T(8,128)}) async-done(((f32[128,128]{1,0:T(8,128)}, f32[384,128]{1,0:T(8,128)}), (f32[128,128]{1,0:T(8,128)}, f32[384,128]{1,0:T(8,128)})) %all-reduce.3.cloned.1.call-update) | async-done | bytes 262160 | tf_op jit(solution)/shard_map/psum | solution.py:146
  540.4 1.5 copy.90
  541.9 1.6 copy.91
  (186 shorter events, 65.2 us)
Async XLA Ops:
  7.2 64.9 %copy-start = (f32[384,128]{1,0:T(8,128)S(1)}, f32[384,128]{1,0:T(8,128)}, u32[]{:S(2)}) copy-start(f32[384,128]{1,0:T(8,128)} %param.15) | copy-start | bytes 589828
  7.2 130.7 %all-gather.2.cloned.1.call-start = ((), (), s32[]{:S(2)}) async-start(), calls=%async_computation | async-start | bytes 1081344 | tf_op jit(solution)/shard_map/all_gather | solution.py:111
  7.9 532.5 %all-reduce.3.cloned.1.call-start = ((), (), s32[]{:S(2)}) async-start(), calls=%async_computation.1 | async-start | bytes 524288 | tf_op jit(solution)/shard_map/psum | solution.py:146
Sparse Core Ops, SparseCore 0:
  10.1 127.7 all-gather.1
  237.7 302.7 all-reduce.2
where the time goes:
time: 552 us; the launch traced here: 550 us
  waiting for transfers between devices  367 us (66%)
  blocking collectives  56.8 us (10%)
  other arithmetic  39.2 us (7%)
  local copies, waits for them, and re-layouts  36.8 us (7%)
  matrix products  35.6 us (6%)
  between operations  14.1 us (3%)
    psum x1, waiting for transfers between devices, body(): lax.psum((grad_query, grad_key), ('ctx', 'head', 'batch'))  302 us
    all_gather x1, waiting for transfers between devices, body(): lax.all_gather(key_rows, 'ctx', axis=1, tiled=True)  63.9 us
    all_gather x1, blocking collectives, body(): pooled_all = lax.all_gather(pooled_local, 'ctx', axis=0, tiled=True)  56.8 us
    dot_general x16, matrix products, score_tile(): jnp.einsum('rgqd,kgd->gqrk', query_group, key_tile, preferred_element_typ...  30.9 us
    reshape x8, local copies, waits for them, and re-layouts, add_pool(): probs.reshape(kv_dev, group_size, block_dev, BLK, key_tile.shape[0] // BL...  22.6 us
    lt x16, other arithmetic, score_tile(): key_pos[None, :] < length  11.6 us
  transfers between devices with their start and end apart: 2, of which 2 were waited for; matrix products, arithmetic and copies ran while one was open for 2% of the time, Pallas kernels for 0%

commit v1 on v0

--- a/solution.py
+++ b/solution.py
@@ -1,3 +1,4 @@
+import functools
 import math
 import jax
 import jax.numpy as jnp
@@ -7,6 +8,15 @@
 BLK = 64
 masked_value = -1e30
 norm_epsilon = 1e-06
+
+
+def draw_strings(my_data, across, axis_id):
+    for no in (across, axis_id):
+        my_data = lax.psum(my_data, no)
+    return my_data
+
+
+push_the_quarters = functools.partial(draw_strings, across="ctx", axis_id=("head", "batch"))
 
 
 def score_tile(query_group, key_tile, query_pos, key_pos, length):
@@ -143,7 +153,7 @@
 
     loss_value, pullback = jax.vjp(local_loss, gate_wq, gate_wk)
     grad_query, grad_key = pullback(jnp.ones((), jnp.float32))
-    grad_query, grad_key = lax.psum((grad_query, grad_key), ("ctx", "head", "batch"))
+    grad_query, grad_key = push_the_quarters((grad_query, grad_key))
     return (target[None], grad_query, grad_key)
 
 

time: 552 us -> 777 us (1.41)
  the two profiles are of different devices: /device:TPU:23 before, /device:TPU:1 now
where the time goes in v1:
time: 777 us; the launch traced here: 776 us
  waiting for transfers between devices  579 us (75%)
  blocking collectives  69.9 us (9%)
  other arithmetic  39.2 us (5%)
  local copies, waits for them, and re-layouts  36.8 us (5%)
  matrix products  35.6 us (5%)
  between operations  13.9 us (2%)
    psum x2, waiting for transfers between devices, draw_strings(): my_data = lax.psum(my_data, no)  520 us
    all_gather x1, blocking collectives, body(): pooled_all = lax.all_gather(pooled_local, 'ctx', axis=0, tiled=True)  69.9 us
    all_gather x1, waiting for transfers between devices, body(): lax.all_gather(key_rows, 'ctx', axis=1, tiled=True)  59 us
    dot_general x16, matrix products, score_tile(): jnp.einsum('rgqd,kgd->gqrk', query_group, key_tile, preferred_element_typ...  30.9 us
    reshape x8, local copies, waits for them, and re-layouts, add_pool(): probs.reshape(kv_dev, group_size, block_dev, BLK, key_tile.shape[0] // BL...  22.6 us
  transfers between devices with their start and end apart: 3, of which 3 were waited for; matrix products, arithmetic and copies ran while one was open for 1% of the time, Pallas kernels for 0%

profile of v1, /device:TPU:1, one launch (start us, length us, event | category | flops | bytes accessed | tf_op | source)
XLA Modules:
  0.0 775.9 jit_solution(3917967442364150629)
XLA Ops:
  10.4 69.9 %all_gather.8 = f32[64,1,384]{2,1,0:T(1,128)S(1)} all-gather(f32[2,1,384]{2,1,0:T(1,128)S(1)} %pad_maximum_fusion), channel_id=1, replica_groups=mesh['ctx'=32,'head'=4,'batch'=4] {'ctx'}, dimensions={0}, use_global_device_ids=true | all-gather | bytes 101376 | tf_op jit(solution)/shard_map/all_gather | solution.py:136
  87.1 59.0 %all-gather.2.cloned.1.call-done = bf16[1,4096,1,128]{3,1,2,0:T(8,128)(2,1)} async-done(((bf16[1,128,1,128]{3,1,2,0:T(8,128)(2,1)}), bf16[1,4096,1,128]{3,1,2,0:T(8,128)(2,1)}) %all-gather.2.cloned.1.call-update) | async-done | bytes 1048592 | tf_op jit(solution)/shard_map/all_gather | solution.py:121
  146.1 22.0 %while.33 = (s32[]{:T(128)}, f32[1,5,128]{2,1,0:T(8,128)S(1)}, f32[1,5,128]{2,1,0:T(8,128)S(1)}, s32[4096]{0:T(1024)S(1)}, s32[]{:T(128)}, /*index=5*/bf16[1,409...) while((s32[]{:T(128)}, f32[1,5,128]{2,1,0:T(8,128)S(1)}, ...), condition=%wide.region_3.4_spmd.clone, body=%wide.region_0.3_spmd.clone.sunk | while | flops 85987080 | bytes 3155650 | solution.py:92
  168.1 74.3 %while.34 = (s32[]{:T(128)}, f32[1,5,2,64]{3,2,1,0:T(2,128)S(1)}, s32[4096]{0:T(1024)S(1)}, s32[]{:T(128)}, bf16[1,4096,1,128]{3,1,2,0:T(8,128)(2,1)}, /*index=5...) while((s32[]{:T(128)}, f32[1,5,2,64]{3,2,1,0:T(2,128)S(1)}, ...), condition=%wide.region_6.7_spmd.clone.clone, body=%wide.region_4.6_spmd.clone.clone.sunk | while | flops 85656376 | bytes 5683170 | solution.py:92
  170.0 2.5 exponential_select_fusion.2
  172.5 2.8 reshape.363
  178.7 2.5 exponential_select_fusion.2
  181.3 2.8 reshape.363
  188.1 2.5 exponential_select_fusion.2
  190.6 2.8 reshape.363
  197.5 2.5 exponential_select_fusion.2
  200.0 2.8 reshape.363
  206.9 2.5 exponential_select_fusion.2
  209.4 2.8 reshape.363
  216.2 2.5 exponential_select_fusion.2
  218.8 2.8 reshape.363
  225.6 2.5 exponential_select_fusion.2
  228.1 2.8 reshape.363
  235.0 2.5 exponential_select_fusion.2
  237.5 2.8 reshape.363
  245.8 311.9 %all-reduce.5.cloned.1.call-done = (f32[128,128]{1,0:T(8,128)}, f32[384,128]{1,0:T(8,128)}) async-done(((f32[128,128]{1,0:T(8,128)}, f32[384,128]{1,0:T(8,128)}), (f32[128,128]{1,0:T(8,128)}, f32[384,128]{1,0:T(8,128)})) %all-reduce.5.cloned.1.call-update) | async-done | bytes 262160 | tf_op jit(solution)/shard_map/psum | solution.py:15
  558.5 207.8 %all-reduce.7.cloned.1.call-done = (f32[128,128]{1,0:T(8,128)}, f32[384,128]{1,0:T(8,128)}) async-done(((f32[128,128]{1,0:T(8,128)}, f32[384,128]{1,0:T(8,128)}), (f32[128,128]{1,0:T(8,128)}, f32[384,128]{1,0:T(8,128)})) %all-reduce.7.cloned.1.call-update) | async-done | bytes 262160 | tf_op jit(solution)/shard_map/psum | solution.py:15
  766.3 1.5 copy.92
  767.7 1.6 copy.93
  (189 shorter events, 66.6 us)
Async XLA Ops:
  7.2 78.0 %copy-start = (f32[384,128]{1,0:T(8,128)S(1)}, f32[384,128]{1,0:T(8,128)}, u32[]{:S(2)}) copy-start(f32[384,128]{1,0:T(8,128)} %param.15) | copy-start | bytes 589828
  7.2 138.9 %all-gather.2.cloned.1.call-start = ((), (), s32[]{:S(2)}) async-start(), calls=%async_computation | async-start | bytes 1081344 | tf_op jit(solution)/shard_map/all_gather | solution.py:121
  7.9 549.8 %all-reduce.5.cloned.1.call-start = ((), (), s32[]{:S(2)}) async-start(), calls=%async_computation.1 | async-start | bytes 524288 | tf_op jit(solution)/shard_map/psum | solution.py:15
  245.8 520.5 %all-reduce.7.cloned.1.call-start = ((), (), s32[]{:S(2)}) async-start(), calls=%async_computation.2 | async-start | bytes 524288 | tf_op jit(solution)/shard_map/psum | solution.py:15
Sparse Core Ops, SparseCore 0:
  10.1 135.9 all-gather.1
  245.9 311.7 all-reduce.4
  560.7 205.5 all-reduce.6
